TPU v7x, 512 devices: a whole 4x8x8 slice. The times are simulated.
512 devices in a mesh: row: 16 (over z, y_lo), col: 32 (over x, y_hi, core).
Axes of the slice: x: 4, y: 8 (y_hi: 4, y_lo: 2; y = y_hi * 2 + y_lo), z: 8, core: 2. Of those that a mesh axis runs over, the one named last changes fastest.
Arguments:
- green_blocks: bfloat16 [16, 32, 12, 2, 288, 288], P('row', 'col'), may hold values from -0.0625 to 0.0625
- slot_rows: int32 [16, 32, 12], P('row', 'col'), may hold values from 0 to 7, as said below
- slot_cols: int32 [16, 32, 12], P('row', 'col'), may hold values from 0 to 3
- slot_count: int32 [16, 32], P('row', 'col'), may hold values from 2 to 12, as said below
- cell_class: int32 [4, 32, 96], P(None, 'col'), may hold values from 0 to 15
- class_contrast: float32 [16, 2], replicated, may hold values from -0.6 to 0.6
- background: float32 [2, 32, 4, 32, 288], P(None, None, None, 'col'), may hold values from -6 to 6
Outputs:
- total_field: float32 [2, 32, 4, 32, 288], P(None, None, None, 'col')
Inputs may be any that keep to these rules, and one draw needn't show every extreme that they name: slot_rows[r, c, s] and slot_cols[r, c, s] name different block pairs within one device's slots, and every slot, used or not, names a block in the upper triangle: (slot_rows // 2) * 32 + 2 r + slot_rows % 2 is at most slot_cols * 32 + c. Slots from slot_count[r, c] on are not used. `slot_count`: some device holds exactly 12 stored blocks.
All inputs are finite; a program needn't handle non-finite values.
Results may differ from a plain program's by a relative error of at most 0.0033.
Values may be sent and summed in bfloat16 or wider, within the bound.
A program may use at most 64 MiB of HBM per device.

v0:
```python
import jax
import jax.numpy as jnp
from jax import lax
from jax.sharding import PartitionSpec as P

PRODUCTS = 3


def from_root(array, axis, root):
    mine = lax.axis_index(axis) == root
    return lax.psum(jnp.where(mine, array, jnp.zeros_like(array)), axis)


def complex_scale(field_now, contrast_re, contrast_im):
    real_part = field_now[0]
    imag_part = field_now[1]
    scaled = jnp.stack(
        [
            contrast_re * real_part - contrast_im * imag_part,
            contrast_re * imag_part + contrast_im * real_part,
        ]
    )
    return scaled.astype(jnp.bfloat16)


def combine(products):
    return jnp.stack([products[0, 0] - products[1, 1], products[0, 1] + products[1, 0]])


def local(green_blocks, slot_rows, slot_cols, slot_count, cell_class, class_contrast, background):
    row_index = lax.axis_index("row")
    col_index = lax.axis_index("col")
    stride = lax.axis_size("col")
    green_tiles = green_blocks[0, 0]
    slot_total = green_tiles.shape[0]
    entries = green_tiles.shape[-1]
    sources = background.shape[1]
    col_blocks = background.shape[2]
    row_blocks = 2 * col_blocks
    local_rows = slot_rows[0, 0]
    local_cols = slot_cols[0, 0]
    global_rows = local_rows // 2 * stride + 2 * row_index + local_rows % 2
    global_cols = local_cols * stride + col_index
    off_diagonal = (global_rows != global_cols).astype(jnp.float32)
    living = (jnp.arange(slot_total) < slot_count[0, 0]).astype(jnp.float32)
    row_pick = (local_rows[:, None] == jnp.arange(row_blocks)[None, :]).astype(
        jnp.float32
    ) * living[:, None]
    col_pick = (local_cols[:, None] == jnp.arange(col_blocks)[None, :]).astype(jnp.float32) * (
        living * off_diagonal
    )[:, None]
    classes = class_contrast.shape[0]
    lookup = (cell_class[:, 0, :, None] == jnp.arange(classes)[None, None, :]).astype(jnp.float32)
    values = jnp.einsum("bte,ec->btc", lookup, class_contrast, precision=lax.Precision.HIGHEST)
    contrast_re = jnp.tile(values[:, :, 0], (1, 3))
    contrast_im = jnp.tile(values[:, :, 1], (1, 3))
    start_field = background[:, :, :, 0, :]
    field_now = start_field
    current = complex_scale(field_now, contrast_re, contrast_im)
    for step_index in range(PRODUCTS):
        final_step = step_index + 1 == PRODUCTS
        halves = [from_root(current, "col", 2 * row_index + parity) for parity in range(2)]
        row_current = jnp.stack(halves, axis=3).reshape(2, sources, row_blocks, entries)
        direct_in = jnp.take(current, local_cols, axis=2)
        mirror_in = jnp.take(row_current, local_rows, axis=2)
        direct_terms = combine(
            jnp.einsum(
                "sqoi,pksi->qpkso", green_tiles, direct_in, preferred_element_type=jnp.float32
            )
        )
        mirror_terms = combine(
            jnp.einsum(
                "sqoi,pkso->qpksi", green_tiles, mirror_in, preferred_element_type=jnp.float32
            )
        )
        direct_part = jnp.einsum(
            "pkse,sb->pkbe", direct_terms, row_pick, precision=lax.Precision.HIGHEST
        )
        mirror_part = jnp.einsum(
            "pkse,sb->pkbe", mirror_terms, col_pick, precision=lax.Precision.HIGHEST
        )
        row_total = lax.psum(direct_part, "col")
        owned_part = lax.dynamic_index_in_dim(
            row_total.reshape(2, sources, col_blocks, 2, entries),
            col_index % 2,
            axis=3,
            keepdims=False,
        )
        direct_here = from_root(owned_part, "row", col_index // 2)
        column_total = lax.psum(mirror_part, "row")
        field_now = start_field + column_total + direct_here
        if not final_step:
            current = complex_scale(field_now, contrast_re, contrast_im)
    return field_now[:, :, :, None, :]


def solution(mesh):
    in_specs = (
        P("row", "col", None, None, None, None),
        P("row", "col", None),
        P("row", "col", None),
        P("row", "col"),
        P(None, "col", None),
        P(),
        P(None, None, None, "col", None),
    )
    out_specs = P(None, None, None, "col", None)
    return jax.shard_map(local, mesh=mesh, in_specs=in_specs, out_specs=out_specs, check_vma=False)
```

profile of v0, /device:TPU:2, one launch (start us, length us, event | category | flops | bytes accessed | tf_op | source)
XLA Modules:
  0.0 2183.8 jit_solution(12541447128961993889)
XLA Ops:
  11.5 4.6 fusion.15
  17.0 1.5 fusion.42
  18.8 1.5 copy.43
  20.4 263.5 %all-reduce.32.cloned.1.call-done = (bf16[2,32,4,1,288]{4,2,1,0,3:T(4,128)(2,1)}, bf16[2,32,4,1,288]{4,2,1,0,3:T(4,128)(2,1)}) async-done(((bf16[2,32,4,1,288]{4,2,1,0,3:T(4,128)(2,1)}, bf16[2,32,4,1,288]{4,2,1,0,3:T(4,128)(2,1)}), (bf16[2,32,4,1,288]{4,2,1,0,3:T(4,128)(2,1)}, bf16[2,32,4,1,288]{4,2,1,0,3:T(4,128)(2,1)})) %all-reduce.32.cloned.1.call-update) | async-done | bytes 294928 | tf_op jit(solution)/shard_map/psum | solution.py:11
  283.9 1.3 pad_maximum_fusion.6
  286.0 3.8 fusion.12
  290.0 2.3 fusion.51
  292.4 278.5 %all-reduce.16.cloned.1.call-done = f32[2,32,4,2,288]{4,2,1,0,3:T(4,128)} async-done(((f32[2,32,4,2,288]{4,2,1,0,3:T(4,128)}), f32[2,32,4,2,288]{4,2,1,0,3:T(4,128)}) %all-reduce.16.cloned.1.call-update) | async-done | bytes 589840 | tf_op jit(solution)/shard_map/psum | solution.py:82
  570.9 1.8 select_bitcast_fusion.2
  572.8 157.6 %all-reduce.26.cloned.1.call-done = (f32[2,32,4,288]{3,2,1,0:T(4,128)}, f32[2,32,4,288]{3,2,1,0:T(4,128)}) async-done(((f32[2,32,4,288]{3,2,1,0:T(4,128)}, f32[2,32,4,288]{3,2,1,0:T(4,128)}), (f32[2,32,4,288]{3,2,1,0:T(4,128)}, f32[2,32,4,288]{3,2,1,0:T(4,128)})) %all-reduce.26.cloned.1.call-update) | async-done | bytes 589840 | tf_op jit(solution)/shard_map/psum | solution.py:11
  730.4 1.3 fusion.96
  733.6 4.6 fusion.21
  738.7 1.5 fusion.45
  740.4 1.5 copy.53
  741.9 264.5 %all-reduce.30.cloned.1.call-done = (bf16[2,32,4,1,288]{4,2,1,0,3:T(4,128)(2,1)}, bf16[2,32,4,1,288]{4,2,1,0,3:T(4,128)(2,1)}) async-done(((bf16[2,32,4,1,288]{4,2,1,0,3:T(4,128)(2,1)}, bf16[2,32,4,1,288]{4,2,1,0,3:T(4,128)(2,1)}), (bf16[2,32,4,1,288]{4,2,1,0,3:T(4,128)(2,1)}, bf16[2,32,4,1,288]{4,2,1,0,3:T(4,128)(2,1)})) %all-reduce.30.cloned.1.call-update) | async-done | bytes 294928 | tf_op jit(solution)/shard_map/psum | solution.py:11
  1006.4 1.3 pad_maximum_fusion.7
  1008.4 3.8 fusion.18
  1012.5 2.3 fusion.54
  1014.8 278.1 %all-reduce.18.cloned.1.call-done = f32[2,32,4,2,288]{4,2,1,0,3:T(4,128)} async-done(((f32[2,32,4,2,288]{4,2,1,0,3:T(4,128)}), f32[2,32,4,2,288]{4,2,1,0,3:T(4,128)}) %all-reduce.18.cloned.1.call-update) | async-done | bytes 589840 | tf_op jit(solution)/shard_map/psum | solution.py:82
  1292.9 1.8 select_bitcast_fusion.1
  1294.8 157.7 %all-reduce.24.cloned.1.call-done = (f32[2,32,4,288]{3,2,1,0:T(4,128)}, f32[2,32,4,288]{3,2,1,0:T(4,128)}) async-done(((f32[2,32,4,288]{3,2,1,0:T(4,128)}, f32[2,32,4,288]{3,2,1,0:T(4,128)}), (f32[2,32,4,288]{3,2,1,0:T(4,128)}, f32[2,32,4,288]{3,2,1,0:T(4,128)})) %all-reduce.24.cloned.1.call-update) | async-done | bytes 589840 | tf_op jit(solution)/shard_map/psum | solution.py:11
  1452.5 1.3 fusion.97
  1455.6 4.6 fusion.27
  1460.6 1.5 fusion.48
  1462.3 1.5 copy.63
  1464.1 264.4 %all-reduce.28.cloned.1.call-done = (bf16[2,32,4,1,288]{4,2,1,0,3:T(4,128)(2,1)}, bf16[2,32,4,1,288]{4,2,1,0,3:T(4,128)(2,1)}) async-done(((bf16[2,32,4,1,288]{4,2,1,0,3:T(4,128)(2,1)}, bf16[2,32,4,1,288]{4,2,1,0,3:T(4,128)(2,1)}), (bf16[2,32,4,1,288]{4,2,1,0,3:T(4,128)(2,1)}, bf16[2,32,4,1,288]{4,2,1,0,3:T(4,128)(2,1)})) %all-reduce.28.cloned.1.call-update) | async-done | bytes 294928 | tf_op jit(solution)/shard_map/psum | solution.py:11
  1730.5 3.8 fusion.24
  1734.6 2.3 fusion.57
  1736.9 278.5 %all-reduce.20.cloned.1.call-done = f32[2,32,4,2,288]{4,2,1,0,3:T(4,128)} async-done(((f32[2,32,4,2,288]{4,2,1,0,3:T(4,128)}), f32[2,32,4,2,288]{4,2,1,0,3:T(4,128)}) %all-reduce.20.cloned.1.call-update) | async-done | bytes 589840 | tf_op jit(solution)/shard_map/psum | solution.py:82
  2015.4 1.8 select_bitcast_fusion
  2017.3 157.5 %all-reduce.22.cloned.1.call-done = (f32[2,32,4,288]{3,2,1,0:T(4,128)}, f32[2,32,4,288]{3,2,1,0:T(4,128)}) async-done(((f32[2,32,4,288]{3,2,1,0:T(4,128)}, f32[2,32,4,288]{3,2,1,0:T(4,128)}), (f32[2,32,4,288]{3,2,1,0:T(4,128)}, f32[2,32,4,288]{3,2,1,0:T(4,128)})) %all-reduce.22.cloned.1.call-update) | async-done | bytes 589840 | tf_op jit(solution)/shard_map/psum | solution.py:11
  2174.8 1.3 fusion.99
  (80 shorter events, 15.8 us)
Async XLA Ops:
  6.5 0.7 copy-start
  6.5 4.2 copy-start.3
  6.5 4.2 copy-start.2
  6.5 277.4 %all-reduce.32.cloned.1.call-start = ((), (), s32[]{:S(2)}) async-start(), calls=%async_computation.8 | async-start | bytes 786432 | tf_op jit(solution)/shard_map/psum | solution.py:11
  10.7 560.2 %all-reduce.16.cloned.1.call-start = ((), (), s32[]{:S(2)}) async-start(), calls=%async_computation | async-start | bytes 1572864 | tf_op jit(solution)/shard_map/psum | solution.py:82
  20.2 710.1 %all-reduce.26.cloned.1.call-start = ((), (), s32[]{:S(2)}) async-start(), calls=%async_computation.5 | async-start | bytes 1572864 | tf_op jit(solution)/shard_map/psum | solution.py:11
  290.0 440.4 %copy-start.1 = (f32[2,32,4,1,288]{4,3,2,1,0:T(1,128)S(1)}, f32[2,32,4,1,288]{4,3,2,1,0:T(1,128)}, u32[]{:S(2)}) copy-start(f32[2,32,4,1,288]{4,3,2,1,0:T(1,128)} %param.17) | copy-start | bytes 884740
  572.7 433.6 %all-reduce.30.cloned.1.call-start = ((), (), s32[]{:S(2)}) async-start(), calls=%async_computation.7 | async-start | bytes 786432 | tf_op jit(solution)/shard_map/psum | solution.py:11
  738.4 554.6 %all-reduce.18.cloned.1.call-start = ((), (), s32[]{:S(2)}) async-start(), calls=%async_computation.1 | async-start | bytes 1572864 | tf_op jit(solution)/shard_map/psum | solution.py:82
  741.9 710.6 %all-reduce.24.cloned.1.call-start = ((), (), s32[]{:S(2)}) async-start(), calls=%async_computation.4 | async-start | bytes 1572864 | tf_op jit(solution)/shard_map/psum | solution.py:11
  1294.8 433.7 %all-reduce.28.cloned.1.call-start = ((), (), s32[]{:S(2)}) async-start(), calls=%async_computation.6 | async-start | bytes 786432 | tf_op jit(solution)/shard_map/psum | solution.py:11
  1460.5 555.0 %all-reduce.20.cloned.1.call-start = ((), (), s32[]{:S(2)}) async-start(), calls=%async_computation.2 | async-start | bytes 1572864 | tf_op jit(solution)/shard_map/psum | solution.py:82
  1463.8 711.0 %all-reduce.22.cloned.1.call-start = ((), (), s32[]{:S(2)}) async-start(), calls=%async_computation.3 | async-start | bytes 1572864 | tf_op jit(solution)/shard_map/psum | solution.py:11
Sparse Core Ops, SparseCore 0:
  10.8 273.0 all-reduce.31
  287.1 283.7 all-reduce.15
  573.8 156.5 all-reduce.25
  738.5 267.8 all-reduce.29
  1009.1 283.7 all-reduce.17
  1296.0 156.4 all-reduce.23
  1460.6 267.8 all-reduce.27
  1731.6 283.7 all-reduce.19
  2018.4 156.3 all-reduce.21
where the time goes:
time: 2180 us
  waiting for transfers between devices  2100 us (96%)
  matrix products  37.7 us (2%)
    psum x6, waiting for transfers between devices, from_root(): return lax.psum(jnp.where(mine, array, jnp.zeros_like(array)), axis)  1270 us
    psum x3, waiting for transfers between devices, local(): row_total = lax.psum(direct_part, 'col')  835 us
  transfers between devices with their start and end apart: 9, of which 9 were waited for; matrix products, arithmetic and copies ran while one was open for 2% of the time, Pallas kernels for 0%

commit v1 on v0

--- a/solution.py
+++ b/solution.py
@@ -79,7 +79,8 @@
         mirror_part = jnp.einsum(
             "pkse,sb->pkbe", mirror_terms, col_pick, precision=lax.Precision.HIGHEST
         )
-        row_total = lax.psum(direct_part, "col")
+        pieces = lax.all_gather(direct_part, "col")
+        row_total = jnp.sum(pieces, axis=0)
         owned_part = lax.dynamic_index_in_dim(
             row_total.reshape(2, sources, col_blocks, 2, entries),
             col_index % 2,

time: 2180 us -> 1840 us (0.84)
  waiting for transfers between devices: 2100 us -> 1730 us
  other arithmetic: 18.1 us -> 44 us
    psum x3 -> x0, waiting for transfers between devices: 835 us -> none  [local(): row_total = lax.psum(direct_part, 'col')]
    all_gather x0 -> x3, waiting for transfers between devices: none -> 506 us  [local(): pieces = lax.all_gather(direct_part, 'col')]
    psum x6, waiting for transfers between devices: 1270 us -> 1220 us  [from_root(): return lax.psum(jnp.where(mine, array, jnp.zeros_like(array)), axis)]
    reduce_sum x0 -> x3, other arithmetic: none -> 28.2 us  [local(): row_total = jnp.sum(pieces, axis=0)]
where the time goes in v1:
time: 1840 us
  waiting for transfers between devices  1730 us (94%)
  other arithmetic  44 us (2%)
  matrix products  40.5 us (2%)
    psum x6, waiting for transfers between devices, from_root(): return lax.psum(jnp.where(mine, array, jnp.zeros_like(array)), axis)  1220 us
    all_gather x3, waiting for transfers between devices, local(): pieces = lax.all_gather(direct_part, 'col')  506 us
  transfers between devices with their start and end apart: 9, of which 9 were waited for; matrix products, arithmetic and copies ran while one was open for 2% of the time, Pallas kernels for 0%

profile of v1, /device:TPU:2, one launch (start us, length us, event | category | flops | bytes accessed | tf_op | source)
XLA Modules:
  0.0 1837.7 jit_solution(7577803729780252532)
XLA Ops:
  6.5 1.3 fusion.155
  10.9 4.6 fusion.15
  16.4 2.5 fusion.42
  19.1 264.4 %all-reduce.23.cloned.1.call-done = (bf16[2,32,4,1,288]{4,2,1,0,3:T(4,128)(2,1)}, bf16[2,32,4,1,288]{4,2,1,0,3:T(4,128)(2,1)}) async-done(((bf16[2,32,4,1,288]{4,2,1,0,3:T(4,128)(2,1)}, bf16[2,32,4,1,288]{4,2,1,0,3:T(4,128)(2,1)}), (bf16[2,32,4,1,288]{4,2,1,0,3:T(4,128)(2,1)}, bf16[2,32,4,1,288]{4,2,1,0,3:T(4,128)(2,1)})) %all-reduce.23.cloned.1.call-update) | async-done | bytes 294928 | tf_op jit(solution)/shard_map/psum | solution.py:11
  283.5 1.3 pad_maximum_fusion.6
  285.5 3.8 fusion.12
  289.6 2.3 fusion.51
  291.9 168.7 %all-gather.7.cloned.1.call-done = f32[64,32,8,288]{3,2,1,0:T(8,128)} async-done(((f32[2,32,8,288]{3,2,1,0:T(8,128)}), f32[64,32,8,288]{3,2,1,0:T(8,128)}) %all-gather.7.cloned.1.call-update) | async-done | bytes 18874384 | tf_op jit(solution)/shard_map/all_gather | solution.py:82
  460.5 9.4 reduce_sum.27
  471.3 143.3 %all-reduce.17.cloned.1.call-done = (f32[2,32,4,288]{3,2,1,0:T(4,128)}, f32[2,32,4,288]{3,2,1,0:T(4,128)}) async-done(((f32[2,32,4,288]{3,2,1,0:T(4,128)}, f32[2,32,4,288]{3,2,1,0:T(4,128)}), (f32[2,32,4,288]{3,2,1,0:T(4,128)}, f32[2,32,4,288]{3,2,1,0:T(4,128)})) %all-reduce.17.cloned.1.call-update) | async-done | bytes 589840 | tf_op jit(solution)/shard_map/psum | solution.py:11
  614.6 1.3 fusion.99
  617.8 4.6 fusion.21
  622.9 2.5 fusion.45
  625.5 265.1 %all-reduce.21.cloned.1.call-done = (bf16[2,32,4,1,288]{4,2,1,0,3:T(4,128)(2,1)}, bf16[2,32,4,1,288]{4,2,1,0,3:T(4,128)(2,1)}) async-done(((bf16[2,32,4,1,288]{4,2,1,0,3:T(4,128)(2,1)}, bf16[2,32,4,1,288]{4,2,1,0,3:T(4,128)(2,1)}), (bf16[2,32,4,1,288]{4,2,1,0,3:T(4,128)(2,1)}, bf16[2,32,4,1,288]{4,2,1,0,3:T(4,128)(2,1)})) %all-reduce.21.cloned.1.call-update) | async-done | bytes 294928 | tf_op jit(solution)/shard_map/psum | solution.py:11
  890.6 1.3 pad_maximum_fusion.7
  892.7 3.8 fusion.18
  896.7 2.3 fusion.54
  899.0 168.5 %all-gather.9.cloned.1.call-done = f32[64,32,8,288]{3,2,1,0:T(8,128)} async-done(((f32[2,32,8,288]{3,2,1,0:T(8,128)}), f32[64,32,8,288]{3,2,1,0:T(8,128)}) %all-gather.9.cloned.1.call-update) | async-done | bytes 18874384 | tf_op jit(solution)/shard_map/all_gather | solution.py:82
  1067.5 9.4 reduce_sum.28
  1078.3 143.3 %all-reduce.15.cloned.1.call-done = (f32[2,32,4,288]{3,2,1,0:T(4,128)}, f32[2,32,4,288]{3,2,1,0:T(4,128)}) async-done(((f32[2,32,4,288]{3,2,1,0:T(4,128)}, f32[2,32,4,288]{3,2,1,0:T(4,128)}), (f32[2,32,4,288]{3,2,1,0:T(4,128)}, f32[2,32,4,288]{3,2,1,0:T(4,128)})) %all-reduce.15.cloned.1.call-update) | async-done | bytes 589840 | tf_op jit(solution)/shard_map/psum | solution.py:11
  1221.6 1.3 fusion.100
  1224.7 4.6 fusion.27
  1229.7 2.5 fusion.48
  1232.5 265.1 %all-reduce.19.cloned.1.call-done = (bf16[2,32,4,1,288]{4,2,1,0,3:T(4,128)(2,1)}, bf16[2,32,4,1,288]{4,2,1,0,3:T(4,128)(2,1)}) async-done(((bf16[2,32,4,1,288]{4,2,1,0,3:T(4,128)(2,1)}, bf16[2,32,4,1,288]{4,2,1,0,3:T(4,128)(2,1)}), (bf16[2,32,4,1,288]{4,2,1,0,3:T(4,128)(2,1)}, bf16[2,32,4,1,288]{4,2,1,0,3:T(4,128)(2,1)})) %all-reduce.19.cloned.1.call-update) | async-done | bytes 294928 | tf_op jit(solution)/shard_map/psum | solution.py:11
  1497.6 1.3 pad_maximum_fusion.8
  1499.6 3.8 fusion.24
  1503.7 2.3 fusion.57
  1506.0 168.7 %all-gather.11.cloned.1.call-done = f32[64,32,8,288]{3,2,1,0:T(8,128)} async-done(((f32[2,32,8,288]{3,2,1,0:T(8,128)}), f32[64,32,8,288]{3,2,1,0:T(8,128)}) %all-gather.11.cloned.1.call-update) | async-done | bytes 18874384 | tf_op jit(solution)/shard_map/all_gather | solution.py:82
  1674.6 9.4 reduce_sum.29
  1685.3 143.4 %all-reduce.13.cloned.1.call-done = (f32[2,32,4,288]{3,2,1,0:T(4,128)}, f32[2,32,4,288]{3,2,1,0:T(4,128)}) async-done(((f32[2,32,4,288]{3,2,1,0:T(4,128)}, f32[2,32,4,288]{3,2,1,0:T(4,128)}), (f32[2,32,4,288]{3,2,1,0:T(4,128)}, f32[2,32,4,288]{3,2,1,0:T(4,128)})) %all-reduce.13.cloned.1.call-update) | async-done | bytes 589840 | tf_op jit(solution)/shard_map/psum | solution.py:11
  1828.7 1.3 fusion.102
  1830.0 1.1 copy.94
  (87 shorter events, 14.6 us)
Async XLA Ops:
  6.5 1.3 copy-start
  6.5 3.6 copy-start.3
  6.5 276.9 %all-reduce.23.cloned.1.call-start = ((), (), s32[]{:S(2)}) async-start(), calls=%async_computation.8 | async-start | bytes 786432 | tf_op jit(solution)/shard_map/psum | solution.py:11
  10.0 450.5 %all-gather.7.cloned.1.call-start = ((), (), s32[]{:S(2)}) async-start(), calls=%async_computation | async-start | bytes 25952256 | tf_op jit(solution)/shard_map/all_gather | solution.py:82
  15.6 0.8 copy-start.4
  19.0 595.6 %all-reduce.17.cloned.1.call-start = ((), (), s32[]{:S(2)}) async-start(), calls=%async_computation.5 | async-start | bytes 1572864 | tf_op jit(solution)/shard_map/psum | solution.py:11
  470.1 144.5 %copy-start.2 = (f32[2,32,4,1,288]{4,3,2,1,0:T(1,128)S(1)}, f32[2,32,4,1,288]{4,3,2,1,0:T(1,128)}, u32[]{:S(2)}) copy-start(f32[2,32,4,1,288]{4,3,2,1,0:T(1,128)} %param.17) | copy-start | bytes 884740
  471.2 419.3 %all-reduce.21.cloned.1.call-start = ((), (), s32[]{:S(2)}) async-start(), calls=%async_computation.7 | async-start | bytes 786432 | tf_op jit(solution)/shard_map/psum | solution.py:11
  622.6 444.9 %all-gather.9.cloned.1.call-start = ((), (), s32[]{:S(2)}) async-start(), calls=%async_computation.1 | async-start | bytes 25952256 | tf_op jit(solution)/shard_map/all_gather | solution.py:82
  625.4 596.1 %all-reduce.15.cloned.1.call-start = ((), (), s32[]{:S(2)}) async-start(), calls=%async_computation.4 | async-start | bytes 1572864 | tf_op jit(solution)/shard_map/psum | solution.py:11
  1078.2 419.3 %all-reduce.19.cloned.1.call-start = ((), (), s32[]{:S(2)}) async-start(), calls=%async_computation.6 | async-start | bytes 786432 | tf_op jit(solution)/shard_map/psum | solution.py:11
  1229.5 445.1 %all-gather.11.cloned.1.call-start = ((), (), s32[]{:S(2)}) async-start(), calls=%async_computation.2 | async-start | bytes 25952256 | tf_op jit(solution)/shard_map/all_gather | solution.py:82
  1232.2 596.5 %all-reduce.13.cloned.1.call-start = ((), (), s32[]{:S(2)}) async-start(), calls=%async_computation.3 | async-start | bytes 1572864 | tf_op jit(solution)/shard_map/psum | solution.py:11
  1685.3 145.9 %copy-start.1 = (f32[16,2]{0,1:T(2,128)S(1)}, f32[16,2]{0,1:T(2,128)}, u32[]{:S(2)}) copy-start(f32[16,2]{0,1:T(2,128)} %param.16) | copy-start | bytes 388
Sparse Core Ops, SparseCore 0:
  10.3 273.0 all-reduce.22
  287.0 173.4 all-gather.6
  471.4 143.1 all-reduce.16
  622.7 267.8 all-reduce.20
  894.0 173.4 all-gather.8
  1078.3 143.1 all-reduce.14
  1229.7 267.8 all-reduce.18
  1501.1 173.4 all-gather.10
  1685.4 143.1 all-reduce.12
